TPU v7x, 512 devices: a whole 4x4x16 slice. The times are simulated.
512 devices in a mesh: leaf: 128 (over y, z, core), panel: 4 (over x).
Axes of the slice: x: 4, y: 4, z: 16, core: 2. Of those that a mesh axis runs over, the one named last changes fastest.
Arguments:
- border: bfloat16 [128, 128, 8192], P('leaf', 'panel'), may hold values from -0.046875 to 0.046875
- solution: bfloat16 [128, 128, 128], P('leaf', 'panel'), may hold values from -6 to 6
- winv_top: bfloat16 [4096, 4096], P(None, ('leaf', 'panel')), as said below
- winv_mid: bfloat16 [4096, 8192], P(None, ('leaf', 'panel')), as said below
- coupling: bfloat16 [8192, 4096], P(('leaf', 'panel')), may hold values from -0.0625 to 0.0625
Outputs:
- top_adjoint: float32 [4096, 128], P(('leaf', 'panel'))
- mid_adjoint: float32 [8192, 128], P(('leaf', 'panel'))
Inputs may be any that keep to these rules, and one draw needn't show every extreme that they name: `winv_top`: each 4096 x 4096 block of the factor is lower triangular with a positive diagonal. `winv_mid`: each 4096 x 4096 block of the factor is lower triangular with a positive diagonal.
All inputs are finite; a program needn't handle non-finite values.
Results may differ from a plain program's by a relative error of at most 0.0003.
Values sent between devices are 32-bit elements; how exact they have to be, the bound alone decides.
A program may use at most 64 MiB of HBM per device.

v0:
```python
import jax
import jax.numpy as jnp
from jax import lax
from jax.sharding import PartitionSpec as P


def from_partner(value, axis, stride):
    mask = 2**stride
    pairs = [(source, source ^ mask) for source in range(lax.axis_size(axis))]
    return lax.ppermute(value, axis, pairs)


def split_half(buffer, chosen):
    half_rows = buffer.shape[0] // 2
    kept_half = lax.dynamic_slice_in_dim(buffer, chosen * half_rows, half_rows, 0)
    sent_half = lax.dynamic_slice_in_dim(buffer, (1 - chosen) * half_rows, half_rows, 0)
    return (kept_half, sent_half)


def split_parity(buffer, chosen):
    paired = buffer.reshape(buffer.shape[0] // 2, 2, buffer.shape[1])
    even_rows = paired[:, 0]
    odd_rows = paired[:, 1]
    kept_rows = jnp.where(chosen == 0, even_rows, odd_rows)
    sent_rows = jnp.where(chosen == 0, odd_rows, even_rows)
    return (kept_rows, sent_rows)


def partner_halving(top_part, mid_part, leaf_id, leaf_bits):
    for bit_pos in reversed(range(leaf_bits)):
        chosen = leaf_id >> bit_pos & 1
        outgoing = []
        top_part, sent_top = split_half(top_part, chosen)
        outgoing.append(sent_top)
        if bit_pos < leaf_bits - 1:
            mid_part, sent_mid = split_half(mid_part, chosen)
            outgoing.append(sent_mid)
        received = from_partner(jnp.concatenate(outgoing, 0), "leaf", bit_pos)
        position = 0
        top_part = top_part + received[: top_part.shape[0]]
        position = top_part.shape[0]
        if bit_pos < leaf_bits - 1:
            mid_part = mid_part + received[position:]
    return (top_part, mid_part)


def body(border, solution, winv_top, winv_mid, coupling):
    leaves = lax.axis_size("leaf")
    leaf_bits = leaves.bit_length() - 1
    front_rows = winv_top.shape[0]
    leaf_id = lax.axis_index("leaf")
    contribution = lax.dot_general(
        border[0], solution[0], (((0,), (0,)), ((), ())), preferred_element_type=jnp.float32
    )
    top_part = contribution[:front_rows]
    mid_part = contribution[front_rows:]
    top_block, mid_block = partner_halving(top_part, mid_part, leaf_id, leaf_bits)
    top_block, mid_block = (
        lax.psum_scatter(top_block, "panel", scatter_dimension=0, tiled=True),
        lax.psum_scatter(mid_block, "panel", scatter_dimension=0, tiled=True),
    )
    top_factor = winv_top.astype(jnp.float32)
    top_inner = lax.psum(
        jnp.dot(top_factor, top_block, precision=lax.Precision.HIGHEST), ("leaf", "panel")
    )
    top_adjoint = jnp.dot(top_factor.T, top_inner, precision=lax.Precision.HIGHEST)
    top_whole = lax.all_gather(top_adjoint, ("leaf", "panel"), axis=0, tiled=True)
    couple = coupling.astype(jnp.float32)
    mid_rhs = mid_block - jnp.dot(couple, top_whole, precision=lax.Precision.HIGHEST)
    mid_factor = winv_mid.astype(jnp.float32)
    group_block = jnp.dot(mid_factor, mid_rhs, precision=lax.Precision.HIGHEST)
    for bit_pos in reversed(range(leaf_bits - 1)):
        chosen = leaf_id >> bit_pos & 1
        kept_rows, sent_rows = split_parity(group_block, chosen)
        group_block = kept_rows + from_partner(sent_rows, "leaf", bit_pos)
    group_block = lax.psum(group_block, "panel")
    for bit_pos in range(leaf_bits - 1):
        chosen = leaf_id >> bit_pos & 1
        received = from_partner(group_block, "leaf", bit_pos)
        even_rows = jnp.where(chosen == 0, group_block, received)
        odd_rows = jnp.where(chosen == 0, received, group_block)
        group_block = jnp.stack([even_rows, odd_rows], 1).reshape(
            2 * group_block.shape[0], group_block.shape[1]
        )
    mid_adjoint = jnp.dot(mid_factor.T, group_block, precision=lax.Precision.HIGHEST)
    return (top_adjoint, mid_adjoint)


def solution(mesh):
    placed = (
        P("leaf", "panel", None),
        P("leaf", "panel", None),
        P(None, ("leaf", "panel")),
        P(None, ("leaf", "panel")),
        P(("leaf", "panel"), None),
    )
    return jax.shard_map(
        body,
        mesh=mesh,
        in_specs=placed,
        out_specs=(P(("leaf", "panel"), None), P(("leaf", "panel"), None)),
        check_vma=False,
    )
```

profile of v0, /device:TPU:1, one launch (start us, length us, event | category | flops | bytes accessed | tf_op | source)
XLA Modules:
  0.0 1222.7 jit_solution(14282266658055465502)
XLA Ops:
  20.1 19.9 %collective-permute-done = f32[2048,128]{1,0:T(8,128)} collective-permute-done((f32[2048,128]{1,0:T(8,128)}, f32[2048,128]{1,0:T(8,128)}, u32[]{:S(2)}, u32[]{:S(2)}) %collective-permute-start) | collective-permute-done | bytes 1048608 | tf_op jit(solution)/shard_map/ppermute | solution.py:10
  42.9 6.2 collective-permute-start.1
  49.1 33.1 %collective-permute-done.1 = f32[3072,128]{1,0:T(8,128)} collective-permute-done((f32[3072,128]{1,0:T(8,128)}, f32[3072,128]{1,0:T(8,128)}, u32[]{:S(2)}, u32[]{:S(2)}) %collective-permute-start.1) | collective-permute-done | bytes 1572896 | tf_op jit(solution)/shard_map/ppermute | solution.py:10
  85.1 15.7 %collective-permute-start.2 = (f32[1536,128]{1,0:T(8,128)S(1)}, f32[1536,128]{1,0:T(8,128)S(1)}, u32[]{:S(2)}, u32[]{:S(2)}) collective-permute-start(f32[1536,128]{1,0:T(8,128)S(1)} %pad_maximum_fusion.3), channel_id=1, source_target_pairs={{0,64},{4,68},{8,72},{12,76},{16,80},{20,84},{24,88},{28,92},{32,9... | collective-permute-start | bytes 2359304 | tf_op jit(solution)/shard_map/ppermute | solution.py:10
  100.8 24.3 %collective-permute-done.2 = f32[1536,128]{1,0:T(8,128)S(1)} collective-permute-done((f32[1536,128]{1,0:T(8,128)S(1)}, f32[1536,128]{1,0:T(8,128)S(1)}, u32[]{:S(2)}, u32[]{:S(2)}) %collective-permute-start.2) | collective-permute-done | bytes 786464 | tf_op jit(solution)/shard_map/ppermute | solution.py:10
  126.4 38.8 %collective-permute-start.3 = (f32[768,128]{1,0:T(8,128)S(1)}, f32[768,128]{1,0:T(8,128)S(1)}, u32[]{:S(2)}, u32[]{:S(2)}) collective-permute-start(f32[768,128]{1,0:T(8,128)S(1)} %pad_maximum_fusion.5), channel_id=1, source_target_pairs={{0,32},{4,36},{8,40},{12,44},{16,48},{20,52},{24,56},{28,60},{32,0... | collective-permute-start | bytes 1179656 | tf_op jit(solution)/shard_map/ppermute | solution.py:10
  165.2 38.6 %collective-permute-done.3 = f32[768,128]{1,0:T(8,128)S(1)} collective-permute-done((f32[768,128]{1,0:T(8,128)S(1)}, f32[768,128]{1,0:T(8,128)S(1)}, u32[]{:S(2)}, u32[]{:S(2)}) %collective-permute-start.3) | collective-permute-done | bytes 393248 | tf_op jit(solution)/shard_map/ppermute | solution.py:10
  205.9 9.6 collective-permute-done.4
  226.7 13.1 %all-reduce = f32[32,128]{1,0:T(8,128)S(1)} all-reduce(f32[32,128]{1,0:T(8,128)S(1)} %slice_add_fusion.11), channel_id=2, replica_groups=mesh['leaf'=128,'panel'=4] {'panel'}, use_global_device_ids=true, to_apply=%region_0.0.clone | all-reduce | flops 4096 | bytes 32768
  242.3 481.7 %all-reduce.3.cloned.1.call-done = f32[4096,128]{0,1:T(8,128)} async-done(((f32[4096,128]{0,1:T(8,128)}), f32[4096,128]{0,1:T(8,128)}) %all-reduce.3.cloned.1.call-update) | async-done | bytes 2097168 | tf_op jit(solution)/shard_map/psum | solution.py:63
  727.9 194.9 %all-gather.2.cloned.1.call-done = f32[4096,128]{1,0:T(8,128)} async-done(((f32[8,128]{1,0:T(8,128)}), f32[4096,128]{1,0:T(8,128)}) %all-gather.2.cloned.1.call-update) | async-done | bytes 2097168 | tf_op jit(solution)/shard_map/all_gather | solution.py:67
  936.0 23.3 %collective-permute-done.7 = f32[2048,128]{1,0:T(8,128)S(1)} collective-permute-done((f32[2048,128]{1,0:T(8,128)}, f32[2048,128]{1,0:T(8,128)S(1)}, u32[]{:S(2)}, u32[]{:S(2)}) %collective-permute-start.7) | collective-permute-done | bytes 1048608 | tf_op jit(solution)/shard_map/ppermute | solution.py:10
  961.4 7.0 collective-permute-start.8
  968.4 39.4 %collective-permute-done.8 = f32[1024,128]{1,0:T(8,128)S(1)} collective-permute-done((f32[1024,128]{1,0:T(8,128)S(1)}, f32[1024,128]{1,0:T(8,128)S(1)}, u32[]{:S(2)}, u32[]{:S(2)}) %collective-permute-start.8) | collective-permute-done | bytes 524320 | tf_op jit(solution)/shard_map/ppermute | solution.py:10
  1010.2 16.4 %collective-permute-done.9 = f32[512,128]{1,0:T(8,128)S(1)} collective-permute-done((f32[512,128]{1,0:T(8,128)S(1)}, f32[512,128]{1,0:T(8,128)S(1)}, u32[]{:S(2)}, u32[]{:S(2)}) %collective-permute-start.9) | collective-permute-done | bytes 262176 | tf_op jit(solution)/shard_map/ppermute | solution.py:10
  1026.8 16.1 %collective-permute-start.10 = (f32[256,128]{1,0:T(8,128)S(1)}, f32[256,128]{1,0:T(8,128)S(1)}, u32[]{:S(2)}, u32[]{:S(2)}) collective-permute-start(f32[256,128]{1,0:T(8,128)S(1)} %bitcast.97), channel_id=1, source_target_pairs={{0,16},{4,20},{8,24},{12,28},{16,0},{20,4},{24,8},{28,12},{32,48},... | collective-permute-start | bytes 393224 | tf_op jit(solution)/shard_map/ppermute | solution.py:10
  1052.5 9.6 collective-permute-start.12
  1062.9 11.6 psum.15
  1088.5 8.5 collective-permute-done.15
  1101.1 24.7 %collective-permute-done.16 = f32[512,128]{1,0:T(8,128)S(1)} collective-permute-done((f32[512,128]{1,0:T(8,128)S(1)}, f32[512,128]{1,0:T(8,128)S(1)}, u32[]{:S(2)}, u32[]{:S(2)}) %collective-permute-start.16) | collective-permute-done | bytes 262176 | tf_op jit(solution)/shard_map/ppermute | solution.py:10
  1126.3 7.0 collective-permute-start.17
  1133.3 45.6 %collective-permute-done.17 = f32[1024,128]{1,0:T(8,128)S(1)} collective-permute-done((f32[1024,128]{1,0:T(8,128)S(1)}, f32[1024,128]{1,0:T(8,128)S(1)}, u32[]{:S(2)}, u32[]{:S(2)}) %collective-permute-start.17) | collective-permute-done | bytes 524320 | tf_op jit(solution)/shard_map/ppermute | solution.py:10
  1181.8 24.2 %collective-permute-done.18 = f32[2048,128]{1,0:T(8,128)S(1)} collective-permute-done((f32[2048,128]{1,0:T(8,128)S(1)}, f32[2048,128]{1,0:T(8,128)S(1)}, u32[]{:S(2)}, u32[]{:S(2)}) %collective-permute-start.18) | collective-permute-done | bytes 1048608 | tf_op jit(solution)/shard_map/ppermute | solution.py:10
  1206.3 7.6 copy.72
  (112 shorter events, 89.0 us)
Async XLA Ops:
  8.0 716.0 %all-reduce.3.cloned.1.call-start = ((), (), s32[]{:S(2)}) async-start(), calls=%async_computation.1 | async-start | bytes 4194304 | tf_op jit(solution)/shard_map/psum | solution.py:63
  14.4 25.6 %collective-permute-start = (f32[2048,128]{1,0:T(8,128)}, f32[2048,128]{1,0:T(8,128)}, u32[]{:S(2)}, u32[]{:S(2)}) collective-permute-start(f32[2048,128]{1,0:T(8,128)} %constant_dynamic-slice_fusion.12), channel_id=1, source_target_pairs={{0,256},{4,260},{8,264},{12,268},{16,272},{20,276},{24,280},{28,28... | collective-permute-start | bytes 3145736 | tf_op jit(solution)/shard_map/ppermute | solution.py:10
  42.9 39.3 %collective-permute-start.1 = (f32[3072,128]{1,0:T(8,128)}, f32[3072,128]{1,0:T(8,128)}, u32[]{:S(2)}, u32[]{:S(2)}) collective-permute-start(f32[3072,128]{1,0:T(8,128)} %pad_maximum_fusion.1), channel_id=1, source_target_pairs={{0,128},{4,132},{8,136},{12,140},{16,144},{20,148},{24,152},{28,15... | collective-permute-start | bytes 4718600 | tf_op jit(solution)/shard_map/ppermute | solution.py:10
  85.1 40.0 %collective-permute-start.2 = (f32[1536,128]{1,0:T(8,128)S(1)}, f32[1536,128]{1,0:T(8,128)S(1)}, u32[]{:S(2)}, u32[]{:S(2)}) collective-permute-start(f32[1536,128]{1,0:T(8,128)S(1)} %pad_maximum_fusion.3), channel_id=1, source_target_pairs={{0,64},{4,68},{8,72},{12,76},{16,80},{20,84},{24,88},{28,92},{32,9... | collective-permute-start | bytes 2359304 | tf_op jit(solution)/shard_map/ppermute | solution.py:10
  126.4 77.4 %collective-permute-start.3 = (f32[768,128]{1,0:T(8,128)S(1)}, f32[768,128]{1,0:T(8,128)S(1)}, u32[]{:S(2)}, u32[]{:S(2)}) collective-permute-start(f32[768,128]{1,0:T(8,128)S(1)} %pad_maximum_fusion.5), channel_id=1, source_target_pairs={{0,32},{4,36},{8,40},{12,44},{16,48},{20,52},{24,56},{28,60},{32,0... | collective-permute-start | bytes 1179656 | tf_op jit(solution)/shard_map/ppermute | solution.py:10
  203.9 11.6 collective-permute-start.4
  215.6 5.8 collective-permute-start.5
  221.5 5.2 collective-permute-start.6
  242.2 680.6 %copy-start.7 = (bf16[16,4096]{1,0:T(8,128)(2,1)S(1)}, bf16[16,4096]{1,0:T(8,128)(2,1)}, u32[]{:S(2)}) copy-start(bf16[16,4096]{1,0:T(8,128)(2,1)} %param.9) | copy-start | bytes 393220
  242.2 683.0 %copy-start.5 = (bf16[4096,16]{0,1:T(8,128)(2,1)S(1)}, bf16[4096,16]{0,1:T(8,128)(2,1)}, u32[]{:S(2)}) copy-start(bf16[4096,16]{0,1:T(8,128)(2,1)} %param.8) | copy-start | bytes 393220
  242.2 680.6 %all-gather.2.cloned.1.call-start = ((), (), s32[]{:S(2)}) async-start(), calls=%async_computation.3 | async-start | bytes 2101248 | tf_op jit(solution)/shard_map/all_gather | solution.py:67
  727.2 198.0 %reduce-scatter.2.cloned.1.call-start = ((), (), s32[]{:S(2)}) async-start(), calls=%async_computation.2 | async-start | bytes 40960 | tf_op jit(solution)/shard_map/reduce_scatter | solution.py:60
  932.8 26.5 %collective-permute-start.7 = (f32[2048,128]{1,0:T(8,128)}, f32[2048,128]{1,0:T(8,128)S(1)}, u32[]{:S(2)}, u32[]{:S(2)}) collective-permute-start(f32[2048,128]{1,0:T(8,128)} %bitcast.8), channel_id=1, source_target_pairs={{0,128},{4,132},{8,136},{12,140},{16,144},{20,148},{24,152},{28,15... | collective-permute-start | bytes 3145736 | tf_op jit(solution)/shard_map/ppermute | solution.py:10
  961.4 46.4 %collective-permute-start.8 = (f32[1024,128]{1,0:T(8,128)S(1)}, f32[1024,128]{1,0:T(8,128)S(1)}, u32[]{:S(2)}, u32[]{:S(2)}) collective-permute-start(f32[1024,128]{1,0:T(8,128)S(1)} %bitcast.87), channel_id=1, source_target_pairs={{0,64},{4,68},{8,72},{12,76},{16,80},{20,84},{24,88},{28,92},{32,9... | collective-permute-start | bytes 1572872 | tf_op jit(solution)/shard_map/ppermute | solution.py:10
  1008.3 18.3 %collective-permute-start.9 = (f32[512,128]{1,0:T(8,128)S(1)}, f32[512,128]{1,0:T(8,128)S(1)}, u32[]{:S(2)}, u32[]{:S(2)}) collective-permute-start(f32[512,128]{1,0:T(8,128)S(1)} %bitcast.96), channel_id=1, source_target_pairs={{0,32},{4,36},{8,40},{12,44},{16,48},{20,52},{24,56},{28,60},{32,0... | collective-permute-start | bytes 786440 | tf_op jit(solution)/shard_map/ppermute | solution.py:10
  1026.8 20.5 %collective-permute-start.10 = (f32[256,128]{1,0:T(8,128)S(1)}, f32[256,128]{1,0:T(8,128)S(1)}, u32[]{:S(2)}, u32[]{:S(2)}) collective-permute-start(f32[256,128]{1,0:T(8,128)S(1)} %bitcast.97), channel_id=1, source_target_pairs={{0,16},{4,20},{8,24},{12,28},{16,0},{20,4},{24,8},{28,12},{32,48},... | collective-permute-start | bytes 393224 | tf_op jit(solution)/shard_map/ppermute | solution.py:10
  1047.4 5.0 collective-permute-start.11
  1052.5 10.4 collective-permute-start.12
  1074.4 6.9 collective-permute-start.13
  1081.4 5.0 collective-permute-start.14
  1086.5 10.5 collective-permute-start.15
  1097.3 28.5 %collective-permute-start.16 = (f32[512,128]{1,0:T(8,128)S(1)}, f32[512,128]{1,0:T(8,128)S(1)}, u32[]{:S(2)}, u32[]{:S(2)}) collective-permute-start(f32[512,128]{1,0:T(8,128)S(1)} %bitcast.85), channel_id=1, source_target_pairs={{0,32},{4,36},{8,40},{12,44},{16,48},{20,52},{24,56},{28,60},{32,0... | collective-permute-start | bytes 786440 | tf_op jit(solution)/shard_map/ppermute | solution.py:10
  1126.3 52.6 %collective-permute-start.17 = (f32[1024,128]{1,0:T(8,128)S(1)}, f32[1024,128]{1,0:T(8,128)S(1)}, u32[]{:S(2)}, u32[]{:S(2)}) collective-permute-start(f32[1024,128]{1,0:T(8,128)S(1)} %bitcast.80), channel_id=1, source_target_pairs={{0,64},{4,68},{8,72},{12,76},{16,80},{20,84},{24,88},{28,92},{32,9... | collective-permute-start | bytes 1572872 | tf_op jit(solution)/shard_map/ppermute | solution.py:10
  1179.8 26.1 %collective-permute-start.18 = (f32[2048,128]{1,0:T(8,128)S(1)}, f32[2048,128]{1,0:T(8,128)S(1)}, u32[]{:S(2)}, u32[]{:S(2)}) collective-permute-start(f32[2048,128]{1,0:T(8,128)S(1)} %bitcast.77), channel_id=1, source_target_pairs={{0,128},{4,132},{8,136},{12,140},{16,144},{20,148},{24,152},{28,15... | collective-permute-start | bytes 3145736 | tf_op jit(solution)/shard_map/ppermute | solution.py:10
  (6 other events, 172.1 us)
Sparse Core Ops, SparseCore 0:
  242.3 481.5 all-reduce.2
  729.1 193.6 all-gather.1
Sparse Core Ops, SparseCore 1:
  730.5 23.3 reduce-scatter.1
where the time goes:
time: 1220 us
  waiting for transfers between devices  999 us (82%)
  starting transfers between devices  137 us (11%)
  blocking collectives  24.7 us (2%)
  local copies, waits for them, and re-layouts  17.6 us (1%)
  between operations  16.9 us (1%)
  matrix products  13.9 us (1%)
  other arithmetic  13.5 us (1%)
    psum x1, waiting for transfers between devices, body(): lax.psum(jnp.dot(top_factor, top_block, precision=lax.Precision.HIGHEST),...  482 us
    ppermute x19, waiting for transfers between devices, from_partner(): return lax.ppermute(value, axis, pairs)  323 us
    all_gather x1, waiting for transfers between devices, body(): lax.all_gather(top_adjoint, ('leaf', 'panel'), axis=0, tiled=True)  195 us
    ppermute x19, starting transfers between devices, from_partner(): return lax.ppermute(value, axis, pairs)  136 us
  transfers between devices with their start and end apart: 22, of which 20 were waited for; matrix products, arithmetic and copies ran while one was open for 0% of the time, Pallas kernels for 0%

commit v1 on v0

--- a/solution.py
+++ b/solution.py
@@ -1,7 +1,20 @@
+import functools
 import jax
 import jax.numpy as jnp
 from jax import lax
 from jax.sharding import PartitionSpec as P
+
+
+def serve_circles(row_data, comm_axis):
+    ledger = []
+    for _ in range(lax.axis_size(comm_axis)):
+        ledger.append(row_data)
+    block_last = jnp.stack(ledger, axis=0)
+    lower = lax.all_to_all(block_last, comm_axis, 0, 0)
+    return jnp.concatenate(lower, axis=0)
+
+
+_update_files = functools.partial(serve_circles, comm_axis=("leaf", "panel"))
 
 
 def from_partner(value, axis, stride):
@@ -64,7 +77,7 @@
         jnp.dot(top_factor, top_block, precision=lax.Precision.HIGHEST), ("leaf", "panel")
     )
     top_adjoint = jnp.dot(top_factor.T, top_inner, precision=lax.Precision.HIGHEST)
-    top_whole = lax.all_gather(top_adjoint, ("leaf", "panel"), axis=0, tiled=True)
+    top_whole = _update_files(top_adjoint)
     couple = coupling.astype(jnp.float32)
     mid_rhs = mid_block - jnp.dot(couple, top_whole, precision=lax.Precision.HIGHEST)
     mid_factor = winv_mid.astype(jnp.float32)

time: 1220 us -> 1140 us (0.934)
  waiting for transfers between devices: 999 us -> 927 us
    all_gather x1 -> x0, waiting for transfers between devices: 195 us -> none  [body(): lax.all_gather(top_adjoint, ('leaf', 'panel'), axis=0, tiled=True)]
    all_to_all x0 -> x1, waiting for transfers between devices: none -> 103 us  [serve_circles(): lower = lax.all_to_all(block_last, comm_axis, 0, 0)]
    ppermute x19, starting transfers between devices: 136 us -> 110 us  [from_partner(): return lax.ppermute(value, axis, pairs)]
    ppermute x19, waiting for transfers between devices: 323 us -> 342 us  [from_partner(): return lax.ppermute(value, axis, pairs)]
    all_to_all x0 -> x1, starting transfers between devices: none -> 16.5 us  [serve_circles(): lower = lax.all_to_all(block_last, comm_axis, 0, 0)]
where the time goes in v1:
time: 1140 us
  waiting for transfers between devices  927 us (81%)
  starting transfers between devices  126 us (11%)
  blocking collectives  24.1 us (2%)
  local copies, waits for them, and re-layouts  19.2 us (2%)
  between operations  16.9 us (1%)
  other arithmetic  13.5 us (1%)
  matrix products  11.7 us (1%)
    psum x1, waiting for transfers between devices, body(): lax.psum(jnp.dot(top_factor, top_block, precision=lax.Precision.HIGHEST),...  482 us
    ppermute x19, waiting for transfers between devices, from_partner(): return lax.ppermute(value, axis, pairs)  342 us
    ppermute x19, starting transfers between devices, from_partner(): return lax.ppermute(value, axis, pairs)  110 us
    all_to_all x1, waiting for transfers between devices, serve_circles(): lower = lax.all_to_all(block_last, comm_axis, 0, 0)  103 us
  transfers between devices with their start and end apart: 22, of which 20 were waited for; matrix products, arithmetic and copies ran while one was open for 0% of the time, Pallas kernels for 0%

profile of v1, /device:TPU:1, one launch (start us, length us, event | category | flops | bytes accessed | tf_op | source)
XLA Modules:
  0.0 1138.2 jit_solution(10445743963526704984)
XLA Ops:
  14.4 5.6 collective-permute-start
  20.1 19.9 %collective-permute-done = f32[2048,128]{1,0:T(8,128)} collective-permute-done((f32[2048,128]{1,0:T(8,128)}, f32[2048,128]{1,0:T(8,128)}, u32[]{:S(2)}, u32[]{:S(2)}) %collective-permute-start) | collective-permute-done | bytes 1048608 | tf_op jit(solution)/shard_map/ppermute | solution.py:23
  42.8 6.2 collective-permute-start.1
  49.0 33.1 %collective-permute-done.1 = f32[3072,128]{1,0:T(8,128)} collective-permute-done((f32[3072,128]{1,0:T(8,128)}, f32[3072,128]{1,0:T(8,128)}, u32[]{:S(2)}, u32[]{:S(2)}) %collective-permute-start.1) | collective-permute-done | bytes 1572896 | tf_op jit(solution)/shard_map/ppermute | solution.py:23
  85.1 15.7 %collective-permute-start.2 = (f32[1536,128]{1,0:T(8,128)S(1)}, f32[1536,128]{1,0:T(8,128)S(1)}, u32[]{:S(2)}, u32[]{:S(2)}) collective-permute-start(f32[1536,128]{1,0:T(8,128)S(1)} %pad_maximum_fusion.3), channel_id=1, source_target_pairs={{0,64},{4,68},{8,72},{12,76},{16,80},{20,84},{24,88},{28,92},{32,9... | collective-permute-start | bytes 2359304 | tf_op jit(solution)/shard_map/ppermute | solution.py:23
  100.8 24.3 %collective-permute-done.2 = f32[1536,128]{1,0:T(8,128)S(1)} collective-permute-done((f32[1536,128]{1,0:T(8,128)S(1)}, f32[1536,128]{1,0:T(8,128)S(1)}, u32[]{:S(2)}, u32[]{:S(2)}) %collective-permute-start.2) | collective-permute-done | bytes 786464 | tf_op jit(solution)/shard_map/ppermute | solution.py:23
  126.3 38.8 %collective-permute-start.3 = (f32[768,128]{1,0:T(8,128)S(1)}, f32[768,128]{1,0:T(8,128)S(1)}, u32[]{:S(2)}, u32[]{:S(2)}) collective-permute-start(f32[768,128]{1,0:T(8,128)S(1)} %pad_maximum_fusion.5), channel_id=1, source_target_pairs={{0,32},{4,36},{8,40},{12,44},{16,48},{20,52},{24,56},{28,60},{32,0... | collective-permute-start | bytes 1179656 | tf_op jit(solution)/shard_map/ppermute | solution.py:23
  165.2 38.6 %collective-permute-done.3 = f32[768,128]{1,0:T(8,128)S(1)} collective-permute-done((f32[768,128]{1,0:T(8,128)S(1)}, f32[768,128]{1,0:T(8,128)S(1)}, u32[]{:S(2)}, u32[]{:S(2)}) %collective-permute-start.3) | collective-permute-done | bytes 393248 | tf_op jit(solution)/shard_map/ppermute | solution.py:23
  205.8 9.6 collective-permute-done.4
  226.6 13.1 %all-reduce = f32[32,128]{1,0:T(8,128)S(1)} all-reduce(f32[32,128]{1,0:T(8,128)S(1)} %slice_add_fusion.11), channel_id=2, replica_groups=mesh['leaf'=128,'panel'=4] {'panel'}, use_global_device_ids=true, to_apply=%region_0.0.clone | all-reduce | flops 4096 | bytes 32768
  242.2 481.8 %all-reduce.3.cloned.1.call-done = f32[4096,128]{0,1:T(8,128)} async-done(((f32[4096,128]{0,1:T(8,128)}), f32[4096,128]{0,1:T(8,128)}) %all-reduce.3.cloned.1.call-update) | async-done | bytes 2097168 | tf_op jit(solution)/shard_map/psum | solution.py:76
  728.1 16.5 %all-to-all-start = ((f32[512,8,128]{2,1,0:T(8,128)}), f32[512,8,128]{2,1,0:T(8,128)S(1)}, u32[]{:S(2)}, u32[]{:S(2)}) async-start(f32[512,8,128]{2,1,0:T(8,128)} %stack.38), calls=%async_computation.1 | async-start | bytes 4194304 | tf_op jit(solution)/shard_map/all_to_all | solution.py:13
  745.3 102.6 %all-to-all-done = f32[512,8,128]{2,1,0:T(8,128)S(1)} async-done(((f32[512,8,128]{2,1,0:T(8,128)}), f32[512,8,128]{2,1,0:T(8,128)S(1)}, u32[]{:S(2)}, u32[]{:S(2)}) %all-to-all-start) | async-done | bytes 2097184 | tf_op jit(solution)/shard_map/all_to_all | solution.py:13
  858.2 24.6 %collective-permute-done.7 = f32[2048,128]{1,0:T(8,128)S(1)} collective-permute-done((f32[2048,128]{1,0:T(8,128)}, f32[2048,128]{1,0:T(8,128)S(1)}, u32[]{:S(2)}, u32[]{:S(2)}) %collective-permute-start.7) | collective-permute-done | bytes 1048608 | tf_op jit(solution)/shard_map/ppermute | solution.py:23
  888.2 53.6 %collective-permute-done.8 = f32[1024,128]{1,0:T(8,128)S(1)} collective-permute-done((f32[1024,128]{1,0:T(8,128)S(1)}, f32[1024,128]{1,0:T(8,128)S(1)}, u32[]{:S(2)}, u32[]{:S(2)}) %collective-permute-start.8) | collective-permute-done | bytes 524320 | tf_op jit(solution)/shard_map/ppermute | solution.py:23
  944.2 20.9 %collective-permute-done.9 = f32[512,128]{1,0:T(8,128)S(1)} collective-permute-done((f32[512,128]{1,0:T(8,128)S(1)}, f32[512,128]{1,0:T(8,128)S(1)}, u32[]{:S(2)}, u32[]{:S(2)}) %collective-permute-start.9) | collective-permute-done | bytes 262176 | tf_op jit(solution)/shard_map/ppermute | solution.py:23
  983.2 10.9 psum.15
  994.1 5.7 collective-permute-start.13
  1007.9 8.9 collective-permute-done.15
  1019.6 24.8 %collective-permute-done.16 = f32[512,128]{1,0:T(8,128)S(1)} collective-permute-done((f32[512,128]{1,0:T(8,128)S(1)}, f32[512,128]{1,0:T(8,128)S(1)}, u32[]{:S(2)}, u32[]{:S(2)}) %collective-permute-start.16) | collective-permute-done | bytes 262176 | tf_op jit(solution)/shard_map/ppermute | solution.py:23
  1044.8 7.0 collective-permute-start.17
  1051.8 42.5 %collective-permute-done.17 = f32[1024,128]{1,0:T(8,128)S(1)} collective-permute-done((f32[1024,128]{1,0:T(8,128)S(1)}, f32[1024,128]{1,0:T(8,128)S(1)}, u32[]{:S(2)}, u32[]{:S(2)}) %collective-permute-start.17) | collective-permute-done | bytes 524320 | tf_op jit(solution)/shard_map/ppermute | solution.py:23
  1097.2 24.2 %collective-permute-done.18 = f32[2048,128]{1,0:T(8,128)S(1)} collective-permute-done((f32[2048,128]{1,0:T(8,128)S(1)}, f32[2048,128]{1,0:T(8,128)S(1)}, u32[]{:S(2)}, u32[]{:S(2)}) %collective-permute-start.18) | collective-permute-done | bytes 1048608 | tf_op jit(solution)/shard_map/ppermute | solution.py:23
  1121.7 7.6 copy.72
  (114 shorter events, 84.7 us)
Async XLA Ops:
  8.0 715.9 %all-reduce.3.cloned.1.call-start = ((), (), s32[]{:S(2)}) async-start(), calls=%async_computation.2 | async-start | bytes 4194304 | tf_op jit(solution)/shard_map/psum | solution.py:76
  14.4 25.6 %collective-permute-start = (f32[2048,128]{1,0:T(8,128)}, f32[2048,128]{1,0:T(8,128)}, u32[]{:S(2)}, u32[]{:S(2)}) collective-permute-start(f32[2048,128]{1,0:T(8,128)} %constant_dynamic-slice_fusion.12), channel_id=1, source_target_pairs={{0,256},{4,260},{8,264},{12,268},{16,272},{20,276},{24,280},{28,28... | collective-permute-start | bytes 3145736 | tf_op jit(solution)/shard_map/ppermute | solution.py:23
  42.8 39.3 %collective-permute-start.1 = (f32[3072,128]{1,0:T(8,128)}, f32[3072,128]{1,0:T(8,128)}, u32[]{:S(2)}, u32[]{:S(2)}) collective-permute-start(f32[3072,128]{1,0:T(8,128)} %pad_maximum_fusion.1), channel_id=1, source_target_pairs={{0,128},{4,132},{8,136},{12,140},{16,144},{20,148},{24,152},{28,15... | collective-permute-start | bytes 4718600 | tf_op jit(solution)/shard_map/ppermute | solution.py:23
  85.1 40.0 %collective-permute-start.2 = (f32[1536,128]{1,0:T(8,128)S(1)}, f32[1536,128]{1,0:T(8,128)S(1)}, u32[]{:S(2)}, u32[]{:S(2)}) collective-permute-start(f32[1536,128]{1,0:T(8,128)S(1)} %pad_maximum_fusion.3), channel_id=1, source_target_pairs={{0,64},{4,68},{8,72},{12,76},{16,80},{20,84},{24,88},{28,92},{32,9... | collective-permute-start | bytes 2359304 | tf_op jit(solution)/shard_map/ppermute | solution.py:23
  126.3 113.5 %copy-start.6 = (bf16[4096,8]{0,1:T(8,128)(2,1)S(1)}, bf16[4096,8]{0,1:T(8,128)(2,1)}, u32[]{:S(2)}) copy-start(bf16[4096,8]{0,1:T(8,128)(2,1)} %param.7) | copy-start | bytes 196612
  126.3 77.4 %collective-permute-start.3 = (f32[768,128]{1,0:T(8,128)S(1)}, f32[768,128]{1,0:T(8,128)S(1)}, u32[]{:S(2)}, u32[]{:S(2)}) collective-permute-start(f32[768,128]{1,0:T(8,128)S(1)} %pad_maximum_fusion.5), channel_id=1, source_target_pairs={{0,32},{4,36},{8,40},{12,44},{16,48},{20,52},{24,56},{28,60},{32,0... | collective-permute-start | bytes 1179656 | tf_op jit(solution)/shard_map/ppermute | solution.py:23
  203.9 11.6 %collective-permute-start.4 = (f32[384,128]{1,0:T(8,128)S(1)}, f32[384,128]{1,0:T(8,128)S(1)}, u32[]{:S(2)}, u32[]{:S(2)}) collective-permute-start(f32[384,128]{1,0:T(8,128)S(1)} %pad_maximum_fusion.7), channel_id=1, source_target_pairs={{0,16},{4,20},{8,24},{12,28},{16,0},{20,4},{24,8},{28,12},{32,48},... | collective-permute-start | bytes 589832 | tf_op jit(solution)/shard_map/ppermute | solution.py:23
  215.6 5.8 collective-permute-start.5
  221.4 5.2 collective-permute-start.6
  728.1 119.8 %copy-start.7 = (bf16[16,4096]{1,0:T(8,128)(2,1)S(1)}, bf16[16,4096]{1,0:T(8,128)(2,1)}, u32[]{:S(2)}) copy-start(bf16[16,4096]{1,0:T(8,128)(2,1)} %param.9) | copy-start | bytes 393220
  728.1 119.8 %all-to-all-start = ((f32[512,8,128]{2,1,0:T(8,128)}), f32[512,8,128]{2,1,0:T(8,128)S(1)}, u32[]{:S(2)}, u32[]{:S(2)}) async-start(f32[512,8,128]{2,1,0:T(8,128)} %stack.38), calls=%async_computation.1 | async-start | bytes 4194304 | tf_op jit(solution)/shard_map/all_to_all | solution.py:13
  744.6 104.1 %reduce-scatter.2.cloned.1.call-start = ((), (), s32[]{:S(2)}) async-start(), calls=%async_computation.3 | async-start | bytes 40960 | tf_op jit(solution)/shard_map/reduce_scatter | solution.py:73
  856.3 26.6 %collective-permute-start.7 = (f32[2048,128]{1,0:T(8,128)}, f32[2048,128]{1,0:T(8,128)S(1)}, u32[]{:S(2)}, u32[]{:S(2)}) collective-permute-start(f32[2048,128]{1,0:T(8,128)} %bitcast.9), channel_id=1, source_target_pairs={{0,128},{4,132},{8,136},{12,140},{16,144},{20,148},{24,152},{28,15... | collective-permute-start | bytes 3145736 | tf_op jit(solution)/shard_map/ppermute | solution.py:23
  884.9 56.9 %collective-permute-start.8 = (f32[1024,128]{1,0:T(8,128)S(1)}, f32[1024,128]{1,0:T(8,128)S(1)}, u32[]{:S(2)}, u32[]{:S(2)}) collective-permute-start(f32[1024,128]{1,0:T(8,128)S(1)} %bitcast.91), channel_id=1, source_target_pairs={{0,64},{4,68},{8,72},{12,76},{16,80},{20,84},{24,88},{28,92},{32,9... | collective-permute-start | bytes 1572872 | tf_op jit(solution)/shard_map/ppermute | solution.py:23
  942.2 22.9 %collective-permute-start.9 = (f32[512,128]{1,0:T(8,128)S(1)}, f32[512,128]{1,0:T(8,128)S(1)}, u32[]{:S(2)}, u32[]{:S(2)}) collective-permute-start(f32[512,128]{1,0:T(8,128)S(1)} %bitcast.100), channel_id=1, source_target_pairs={{0,32},{4,36},{8,40},{12,44},{16,48},{20,52},{24,56},{28,60},{32,0... | collective-permute-start | bytes 786440 | tf_op jit(solution)/shard_map/ppermute | solution.py:23
  965.3 7.4 collective-permute-start.10
  972.8 5.0 collective-permute-start.11
  977.9 5.3 collective-permute-start.12
  994.1 6.6 collective-permute-start.13
  1000.8 5.0 collective-permute-start.14
  1005.9 10.8 collective-permute-start.15
  1017.0 27.3 %collective-permute-start.16 = (f32[512,128]{1,0:T(8,128)S(1)}, f32[512,128]{1,0:T(8,128)S(1)}, u32[]{:S(2)}, u32[]{:S(2)}) collective-permute-start(f32[512,128]{1,0:T(8,128)S(1)} %bitcast.89), channel_id=1, source_target_pairs={{0,32},{4,36},{8,40},{12,44},{16,48},{20,52},{24,56},{28,60},{32,0... | collective-permute-start | bytes 786440 | tf_op jit(solution)/shard_map/ppermute | solution.py:23
  1044.8 49.5 %collective-permute-start.17 = (f32[1024,128]{1,0:T(8,128)S(1)}, f32[1024,128]{1,0:T(8,128)S(1)}, u32[]{:S(2)}, u32[]{:S(2)}) collective-permute-start(f32[1024,128]{1,0:T(8,128)S(1)} %bitcast.84), channel_id=1, source_target_pairs={{0,64},{4,68},{8,72},{12,76},{16,80},{20,84},{24,88},{28,92},{32,9... | collective-permute-start | bytes 1572872 | tf_op jit(solution)/shard_map/ppermute | solution.py:23
  1095.3 26.1 %collective-permute-start.18 = (f32[2048,128]{1,0:T(8,128)S(1)}, f32[2048,128]{1,0:T(8,128)S(1)}, u32[]{:S(2)}, u32[]{:S(2)}) collective-permute-start(f32[2048,128]{1,0:T(8,128)S(1)} %bitcast.81), channel_id=1, source_target_pairs={{0,128},{4,132},{8,136},{12,140},{16,144},{20,148},{24,152},{28,15... | collective-permute-start | bytes 3145736 | tf_op jit(solution)/shard_map/ppermute | solution.py:23
  (7 other events, 164.3 us)
Sparse Core Ops, SparseCore 0:
  242.3 481.5 all-reduce.2
Sparse Core Ops, SparseCore 1:
  747.8 29.0 reduce-scatter.1
